TPU v7x, 256 devices: a whole 4x4x8 slice. The times are simulated.
256 devices in a mesh: bl: 32 (over x, z), ta: 8 (over y, core).
Axes of the slice: x: 4, y: 4, z: 8, core: 2. Of those that a mesh axis runs over, the one named last changes fastest.
Arguments:
- log_amplitude: bfloat16 [8192, 8, 1536], P('bl', 'ta'), may hold values from -2.5 to 2.5
- phase: bfloat16 [8192, 8, 1536], P('bl', 'ta'), may hold values from -4 to 4
- redundant_group_index: int32 [8192], P('bl'), may hold values from 0 to 223, as said below
- antenna_couples: int32 [8192, 2], P('bl'), may hold values from 0 to 349, as said below
- tile_flag_mask: int32 [8192, 12], P(('bl', 'ta')), may hold values from 0 to 1, as said below
- inverse: float32 [2, 350, 350], replicated, may hold values from -1 to 1
- integration_kernel: float32 [8, 8], replicated, may hold values from 0.01 to 1
- channel_kernel: bfloat16 [7, 128, 128], replicated, may hold values from 0.0009994507 to 1
Outputs:
- antenna_gains: float32 [2, 350, 8, 1536], P(None, None, 'ta')
- filled: float32 [2, 8192, 8, 1536], P(None, ('bl', 'ta'))
Inputs may be any that keep to these rules, and one draw needn't show every extreme that they name: `redundant_group_index`: every group from 0 to 223 holds at least one baseline. `antenna_couples`: the two antennas of a baseline differ. `tile_flag_mask`: both neighbouring tiles of a flagged tile are unflagged.
All inputs are finite; a program needn't handle non-finite values.
Results may differ from a plain program's by a relative error of at most 0.0029.
Values may be sent and summed in bfloat16 or wider, within the bound.
A program may use at most 64 MiB of HBM per device.

v0:
```python
import jax
import jax.numpy as jnp
from jax import lax
from jax.experimental import pallas as pl
from jax.experimental.pallas import tpu as pltpu
from jax.sharding import PartitionSpec as P

ANTENNA_COUNT = 350
NGRP = 224
TILE = 128
REACH = 3
HIGH = lax.Precision.HIGHEST
F32 = jnp.float32
BF16 = jnp.bfloat16
I16 = jnp.int16
I32 = jnp.int32
MESH = pl.DeviceIdType.MESH

NX, NZ = 4, 8
NBL = NX * NZ
NTA = 8
NT = 8
ROWS = 256
BASE = ROWS // NTA
CH = 1536
PARTS = 3
CW = CH // PARTS
OWN = CW // NBL
APAD = 384
A8 = 352
HOT = NGRP + 2 * A8
NTILE = CH // TILE
PAIR = 2 * TILE
WINDOW = 8 * TILE
EDGE = REACH * TILE
LINE = 2 * BASE


def nt(a, b, precision=None):
    return lax.dot_general(
        a, b, (((1,), (1,)), ((), ())), preferred_element_type=F32, precision=precision
    )


def encode(g):
    peak = jnp.max(jnp.abs(g), axis=1, keepdims=True)
    k = jnp.floor(jnp.log2(jnp.maximum(peak, F32(2.0**-100)))).astype(I32) + 2
    coded = jnp.round(g * jnp.exp2((15 - k).astype(F32))).astype(I32)
    lane = lax.broadcasted_iota(I32, g.shape, 1)
    return jnp.where(lane == ANTENNA_COUNT, k, coded)


def sin_cos(v):
    n = jnp.round(v * F32(0.6366197723675814))
    r = v - n * F32(1.5703125)
    r = r - n * F32(4.837512969970703125e-4)
    r = r - n * F32(7.54978995489188216e-8)
    quadrant = n.astype(I32)
    z = r * r
    s = ((F32(-1.9515295891e-4) * z + F32(8.3321608736e-3)) * z - F32(1.6666654611e-1)) * z * r + r
    c = (
        (F32(2.443315711809948e-5) * z - F32(1.388731625493765e-3)) * z + F32(4.166664568298827e-2)
    ) * z * z - F32(0.5) * z + F32(1.0)
    swap = (quadrant & 1) != 0
    sine = jnp.where(swap, c, s)
    cosine = jnp.where(swap, s, c)
    sine = jnp.where((quadrant & 2) != 0, -sine, sine)
    cosine = jnp.where(((quadrant + 1) & 2) != 0, -cosine, cosine)
    return sine, cosine


def whole_kernel(
    amp, ph, group_row, couples, flags, times, channel, inverse, gains, filled,
    send, got, index, got_index, hot, inv, total, sums, count, shared,
    g_full, g_high, g_low, select, combo, wide, keep, keep_wide, masked, rden, mixed,
    out_cal, in_cal,
    index_send, index_recv, data_send, data_recv, b1_send, b1_recv, b2_send, b2_recv,
    b3_send, b3_recv, cal_send, cal_recv,
):
    me = lax.axis_index("bl")
    mx, mz = me // NZ, lax.rem(me, NZ)
    mt = lax.axis_index("ta")

    def x_of(dx):
        return lax.rem(mx + dx + NX, NX)

    def z_of(dz):
        return lax.rem(mz + dz + NZ, NZ)

    def device(dx, dz):
        return x_of(dx) * NZ + z_of(dz)

    def peer_of(j):
        return device(j // NZ, lax.rem(3 * j, NZ))

    def time_peer(j):
        return lax.rem(mt + j, NTA)

    def remote(src, dst, send_sem, recv_sem, axis, peer):
        return pltpu.make_async_remote_copy(
            src_ref=src, dst_ref=dst, send_sem=send_sem, recv_sem=recv_sem,
            device_id={axis: peer}, device_id_type=MESH,
        )

    def index_copy(j):
        return remote(
            index, got_index.at[j], index_send.at[j], index_recv.at[j], "bl", peer_of(j)
        )

    def data_copy(n, j):
        peer = peer_of(j)
        return remote(
            send.at[n, peer], got.at[n, j], data_send.at[n, j], data_recv.at[n, j], "bl", peer
        )

    def cal_copy(n, j):
        peer = time_peer(j)
        return remote(
            out_cal.at[n, peer], in_cal.at[n, j], cal_send.at[n, j], cal_recv.at[n, j], "ta", peer
        )

    def b1(n, dz, step, half=None):
        slot = shared.at[n, mx, z_of(dz)]
        number = (step - dz) % NZ
        if half is not None:
            slot = slot.at[:, pl.ds(half * APAD, APAD)]
            number = 4 * half
        return remote(slot, slot, b1_send.at[n, number], b1_recv.at[n, number], "bl", device(0, step))

    def b1_wait(n, dz, half=None):
        slot = shared.at[n, mx, z_of(dz)]
        number = (-dz) % NZ
        if half is not None:
            slot = slot.at[:, pl.ds(half * APAD, APAD)]
            number = 4 * half
        remote(slot, slot, b1_send.at[n, number], b1_recv.at[n, number], "bl", device(0, 1)).wait_recv()

    def b2(n, way, dz, src_x):
        slot = shared.at[n, src_x, z_of(dz)]
        number = dz % NZ
        return remote(
            slot, slot, b2_send.at[n, way, number], b2_recv.at[n, way, number],
            "bl", device(1 - 2 * way, 0),
        )

    def b3(n, way, dz, src_x):
        slot = shared.at[n, src_x, z_of(dz)]
        number = dz % NZ
        return remote(
            slot, slot, b3_send.at[n, number], b3_recv.at[n, number], "bl", device(1 - 2 * way, 0)
        )

    barrier = pltpu.get_barrier_semaphore()

    @pl.loop(1, NBL)
    def _(j):
        pl.semaphore_signal(barrier, inc=1, device_id={"bl": peer_of(j)}, device_id_type=MESH)

    @pl.loop(1, NTA)
    def _(j):
        pl.semaphore_signal(barrier, inc=1, device_id={"ta": time_peer(j)}, device_id_type=MESH)

    def turn(n):
        cols = slice(n * CW, (n + 1) * CW)
        send[n, :, 0:OWN, :] = amp[:, cols].T.reshape(NBL, OWN, ROWS)
        send[n, :, OWN:2 * OWN, :] = ph[:, cols].T.reshape(NBL, OWN, ROWS)
        got[n, 0] = send[n, me]

    index[...] = jnp.concatenate(
        [
            ref[k:k + 1, h * TILE:(h + 1) * TILE]
            for ref, k in ((group_row, 0), (couples, 0), (couples, 1)) for h in (0, 1)
        ] + [jnp.zeros((2, TILE), I32)], axis=0
    ).astype(I16)
    turn(0)
    pl.semaphore_wait(barrier, NBL - 1 + NTA - 1)

    @pl.loop(1, NBL)
    def _(j):
        index_copy(j).start()

    @pl.loop(1, NBL)
    def _(j):
        data_copy(0, j).start()

    turn(1)
    turn(2)

    got_index[0] = index[...]
    inv[...] = jnp.zeros_like(inv)
    for s in (0, 1):
        inv[s, 0:ANTENNA_COUNT, 0:ANTENNA_COUNT] = inverse[:, s, :]
    label = lax.broadcasted_iota(I32, (APAD, ROWS), 0)
    first = (couples[0:1, :] == label).astype(F32)
    second = (couples[1:2, :] == label).astype(F32)
    select[0] = (first + second).T.astype(BF16)
    select[1] = (first - second).T.astype(BF16)
    wide[...] = jnp.zeros_like(wide)
    for c in (0, 1):
        for o in range(2 * REACH + 1):
            wide[c * TILE:(c + 1) * TILE, (c + o) * TILE:(c + o + 1) * TILE] = channel[o]
    masked[...] = jnp.zeros_like(masked)
    keep_wide[...] = jnp.zeros_like(keep_wide)
    tile = lax.broadcasted_iota(I32, (NTILE, CH), 1) // TILE
    spread = (tile == lax.broadcasted_iota(I32, (NTILE, CH), 0)).astype(F32).astype(BF16)
    open_tiles = (1 - flags[...]).astype(F32).astype(BF16)
    keep[...] = lax.dot_general(
        open_tiles, spread, (((0,), (0,)), ((), ())), preferred_element_type=F32
    )
    keep_wide[:, EDGE:EDGE + CH] = keep[...].astype(BF16)
    for p in range(NTILE // 2):
        rden[:, PAIR * p:PAIR * (p + 1)] = 1.0 / nt(
            keep_wide[:, PAIR * p:PAIR * p + WINDOW], wide[...]
        )

    def clear(*refs):
        for ref in refs:
            ref[...] = jnp.zeros_like(ref)

    clear(total)

    def add_sums(n, low, high):
        @pl.loop(low, high)
        def _(j):
            @pl.when(j > 0)
            def _():
                if n == 0:
                    index_copy(j).wait_recv()
                data_copy(n, j).wait_recv()
                if n + 1 < PARTS:
                    data_copy(n + 1, j).start()

            d = got[n, j]
            if n == 0:
                ix = got_index[j].astype(I32)

                def one_hot(k, size):
                    row = jnp.concatenate([ix[2 * k:2 * k + 1], ix[2 * k + 1:2 * k + 2]], axis=1)
                    return (lax.broadcasted_iota(I32, (size, ROWS), 0) == row).astype(F32)

                group = one_hot(0, NGRP).astype(BF16)
                one, two = one_hot(1, A8), one_hot(2, A8)
                plus = (one + two).astype(BF16)
                minus = (one - two).astype(BF16)
                hot[j, 0:NGRP] = group
                hot[j, NGRP:NGRP + A8] = plus
                hot[j, NGRP + A8:HOT] = minus
                total[...] += nt(hot[j], jnp.concatenate([group, d], axis=0))
            else:
                sums[...] += nt(hot[j], d)

    def solve(n):
        if n == 0:
            sums[...] = total[:, NGRP:NGRP + 2 * OWN]
            count[...] = jnp.broadcast_to(
                jnp.sum(total[0:NGRP, 0:NGRP], axis=1, keepdims=True), (NGRP, 2 * OWN)
            )
        mean = sums[0:NGRP] / count[...]
        for s in (0, 1):
            rows = slice(NGRP + s * A8, NGRP + (s + 1) * A8)
            cols = slice(s * OWN, (s + 1) * OWN)
            rhs = sums[rows, cols] - jnp.dot(
                total[rows, 0:NGRP], mean[:, cols], precision=HIGH, preferred_element_type=F32
            )
            g = nt(rhs.T, inv[s], HIGH)
            shared[n, mx, mz, :, s * APAD:(s + 1) * APAD] = encode(g).astype(I16)
        if n + 1 < PARTS:
            clear(sums)

    started = []

    def begin(copy):
        copy.start()
        started.append(copy)

    def spread_start(n):
        for step in (1, -1, 2, -2):
            begin(b1(n, 0, step))
        for way in (0, 1):
            begin(b2(n, way, 0, mx))

    def spread_near(n):
        for sign in (-1, 1):
            b1_wait(n, 2 * sign)
            begin(b1(n, 2 * sign, -sign))
            begin(b1(n, 2 * sign, -2 * sign, half=0 if sign < 0 else 1))
            b1_wait(n, sign)
        for dz in (-1, 1, -2, 2):
            for way in (0, 1):
                begin(b2(n, way, dz, mx))

    def spread_far(n):
        for dz in (-3, 3):
            b1_wait(n, dz)
            for way in (0, 1):
                begin(b2(n, way, dz, mx))
        for half in (0, 1):
            b1_wait(n, 4, half=half)
        for way in (0, 1):
            begin(b2(n, way, 4, mx))

    order = (0, -1, 1, -2, 2, -3, 3, 4)

    def spread_across(n):
        for i, dz in enumerate(order):
            for way in (0, 1):
                source = x_of(2 * way - 1)
                b2(n, way, dz, source).wait_recv()
                if i % 2 == way:
                    begin(b3(n, way, dz, source))

    def spread_end(n):
        for i, dz in enumerate(order):
            b3(n, i % 2, dz, x_of(2)).wait_recv()

    def calibrate(n):
        @pl.loop(0, NX)
        def _(x):
            rows = pl.ds(pl.multiple_of(x * NZ * OWN, NZ * OWN), NZ * OWN)
            q = shared[n, x].reshape(NZ * OWN, 2 * APAD).astype(I32)
            for s in (0, 1):
                cols = slice(s * APAD, (s + 1) * APAD)
                part = q[:, cols]
                k = part[:, ANTENNA_COUNT:ANTENNA_COUNT + 1] - 15
                g = part.astype(F32) * jnp.exp2(k.astype(F32))
                high = g.astype(BF16)
                g_full[rows, cols] = g
                g_high[rows, cols] = high
                g_low[rows, cols] = (g - high.astype(F32)).astype(BF16)

        for s in (0, 1):
            cols = slice(s * APAD, (s + 1) * APAD)
            combo[s] = nt(select[s], g_high[:, cols]) + nt(select[s], g_low[:, cols])

        @pl.loop(0, NTA)
        def _(d):
            rows = pl.ds(pl.multiple_of(d * BASE, BASE), BASE)
            cols = slice(n * CW, (n + 1) * CW)
            u = amp[rows, cols].astype(F32) - combo[0, rows, :]
            v = ph[rows, cols].astype(F32) - combo[1, rows, :]
            magnitude = jnp.exp(u)
            sine, cosine = sin_cos(v)
            out_cal[n, d, 0] = (magnitude * cosine).astype(BF16)
            out_cal[n, d, 1] = (magnitude * sine).astype(BF16)

        @pl.loop(1, NTA)
        def _(j):
            cal_copy(n, j).start()

        in_cal[n, 0] = out_cal[n, mt]
        for s in (0, 1):
            @pl.loop(0, CW // TILE)
            def _(k):
                block = g_full[pl.ds(pl.multiple_of(k * TILE, TILE), TILE), s * APAD:(s + 1) * APAD]
                start = s * ANTENNA_COUNT * NTILE + n * (CW // TILE) + k
                gains[pl.ds(start, ANTENNA_COUNT, stride=NTILE), :] = block.T[0:ANTENNA_COUNT]

    def mask(n):
        @pl.loop(0, NTA)
        def _(j):
            @pl.when(j > 0)
            def _():
                cal_copy(n, j).wait_recv()

            row = pl.multiple_of(lax.rem(mt - j + NTA, NTA) * LINE, LINE)
            w = keep[:, n * CW:(n + 1) * CW].astype(BF16)
            for c in (0, 1):
                masked[pl.ds(row + c * BASE, BASE), EDGE + n * CW:EDGE + (n + 1) * CW] = (
                    in_cal[n, j, c] * w
                )

    def fill(low, high):
        @pl.loop(low, high)
        def _(p):
            lane = pl.multiple_of(p * PAIR, PAIR)
            mixed[...] = nt(masked[:, pl.ds(lane, WINDOW)], wide[...])

            @pl.loop(0, NT)
            def _(to):
                total = times[to, 0]
                value = times[to, 0] * mixed[0:LINE]
                for t in range(1, NT):
                    total = total + times[to, t]
                    value = value + times[to, t] * mixed[t * LINE:(t + 1) * LINE]
                ratio = rden[:, pl.ds(lane, PAIR)] * (1.0 / jnp.full((1, PAIR), total, F32))
                w = keep[:, pl.ds(lane, PAIR)]
                for c in (0, 1):
                    row = pl.multiple_of(to * LINE + c * BASE, BASE)
                    own = masked[pl.ds(row, BASE), pl.ds(pl.multiple_of(lane + EDGE, TILE), PAIR)]
                    result = jnp.where(
                        w > 0.5, own.astype(F32), value[c * BASE:(c + 1) * BASE] * ratio
                    )
                    for i in (0, 1):
                        start = c * BASE * NTILE * NT + (2 * p + i) * NT + to
                        filled[pl.ds(start, BASE, stride=NTILE * NT), :] = (
                            result[:, i * TILE:(i + 1) * TILE]
                        )

    add_sums(0, 0, NBL)
    solve(0)
    spread_start(0)
    add_sums(1, 0, 8)
    spread_near(0)
    add_sums(1, 8, 16)
    spread_far(0)
    add_sums(1, 16, 24)
    spread_across(0)
    add_sums(1, 24, NBL)
    solve(1)
    spread_start(1)
    spread_end(0)
    add_sums(2, 0, 8)
    spread_near(1)
    calibrate(0)
    add_sums(2, 8, 16)
    spread_far(1)
    add_sums(2, 16, 24)
    spread_across(1)
    add_sums(2, 24, NBL)
    solve(2)
    spread_start(2)
    spread_end(1)
    mask(0)
    spread_near(2)
    calibrate(1)
    spread_far(2)
    spread_across(2)
    mask(1)
    fill(0, 2)
    spread_end(2)
    calibrate(2)
    mask(2)
    fill(2, NTILE // 2)

    for copy in started:
        copy.wait_send()

    @pl.loop(1, NBL)
    def _(j):
        index_copy(j).wait_send()
        for n in range(PARTS):
            data_copy(n, j).wait_send()

    @pl.loop(1, NTA)
    def _(j):
        for n in range(PARTS):
            cal_copy(n, j).wait_send()


def calibrate_and_fill(amp, ph, group_row, couples, flags, times, channel, inverse):
    dma = pltpu.SemaphoreType.DMA
    vmem = pl.BlockSpec(memory_space=pltpu.VMEM)
    smem = pl.BlockSpec(memory_space=pltpu.SMEM)
    return pl.pallas_call(
        whole_kernel,
        name="calibrate_and_fill",
        out_shape=(
            jax.ShapeDtypeStruct((2 * ANTENNA_COUNT * NTILE, TILE), F32),
            jax.ShapeDtypeStruct((2 * BASE * NTILE * NT, TILE), F32),
        ),
        in_specs=[vmem] * 5 + [smem, vmem, vmem],
        out_specs=(vmem, vmem),
        scratch_shapes=[
            pltpu.VMEM((PARTS, NBL, 2 * OWN, ROWS), BF16),
            pltpu.VMEM((PARTS, NBL, 2 * OWN, ROWS), BF16),
            pltpu.VMEM((8, 128), I16),
            pltpu.VMEM((NBL, 8, 128), I16),
            pltpu.VMEM((NBL, HOT, ROWS), BF16),
            pltpu.VMEM((2, APAD, A8), F32),
            pltpu.VMEM((HOT, NGRP + 2 * OWN), F32),
            pltpu.VMEM((HOT, 2 * OWN), F32),
            pltpu.VMEM((NGRP, 2 * OWN), F32),
            pltpu.VMEM((PARTS, NX, NZ, OWN, 2 * APAD), I16),
            pltpu.VMEM((CW, 2 * APAD), F32),
            pltpu.VMEM((CW, 2 * APAD), BF16),
            pltpu.VMEM((CW, 2 * APAD), BF16),
            pltpu.VMEM((2, ROWS, APAD), BF16),
            pltpu.VMEM((2, ROWS, CW), F32),
            pltpu.VMEM((PAIR, WINDOW), BF16),
            pltpu.VMEM((BASE, CH), F32),
            pltpu.VMEM((BASE, CH + 2 * EDGE), BF16),
            pltpu.VMEM((NT * LINE, CH + 2 * EDGE), BF16),
            pltpu.VMEM((BASE, CH), F32),
            pltpu.VMEM((NT * LINE, PAIR), F32),
            pltpu.VMEM((PARTS, NTA, 2, BASE, CW), BF16),
            pltpu.VMEM((PARTS, NTA, 2, BASE, CW), BF16),
            dma((NBL,)), dma((NBL,)), dma((PARTS, NBL)), dma((PARTS, NBL)),
            dma((PARTS, NZ)), dma((PARTS, NZ)), dma((PARTS, 2, NZ)), dma((PARTS, 2, NZ)),
            dma((PARTS, NZ)), dma((PARTS, NZ)), dma((PARTS, NTA)), dma((PARTS, NTA)),
        ],
        compiler_params=pltpu.CompilerParams(
            collective_id=0, has_side_effects=True, vmem_limit_bytes=56 * 2**20
        ),
    )(amp, ph, group_row, couples, flags, times, channel, inverse)


def copy_kernel(a, out):
    out[...] = a[...]


def copy_out(a):
    spec = pl.BlockSpec((a.shape[0] // 10, TILE), lambda i: (i, 0))
    return pl.pallas_call(
        copy_kernel,
        name="copy_out",
        grid=(10,),
        out_shape=jax.ShapeDtypeStruct(a.shape, a.dtype),
        in_specs=[spec],
        out_specs=spec,
    )(a)


def on_device(
    log_amplitude,
    phase,
    redundant_group_index,
    antenna_couples,
    tile_flag_mask,
    inverse,
    integration_kernel,
    channel_kernel,
):
    gains, filled = calibrate_and_fill(
        log_amplitude[:, 0], phase[:, 0], redundant_group_index[None, :], antenna_couples.T,
        tile_flag_mask.T, integration_kernel, channel_kernel, inverse.transpose(1, 0, 2),
    )
    gains = copy_out(gains)
    return (
        gains.reshape(2, ANTENNA_COUNT, 1, CH),
        filled.reshape(2, BASE, NTILE, NT, TILE).transpose(0, 1, 3, 2, 4).reshape(2, BASE, NT, CH),
    )


def solution(mesh):
    in_specs = (
        P("bl", "ta", None),
        P("bl", "ta", None),
        P("bl"),
        P("bl", None),
        P(("bl", "ta"), None),
        P(),
        P(),
        P(),
    )
    out_specs = (P(None, None, "ta", None), P(None, ("bl", "ta"), None, None))
    return jax.shard_map(
        on_device, mesh=mesh, in_specs=in_specs, out_specs=out_specs, check_vma=False
    )
```

profile of v0, /device:TPU:1, one launch (start us, length us, event | category | flops | bytes accessed | tf_op | source)
XLA Modules:
  0.0 125.8 jit_solution(12925115914472031435)
XLA Ops:
  0.6 115.9 %calibrate_and_fill.1 = (f32[8400,128]{1,0:T(8,128)}, f32[6144,128]{1,0:T(8,128)}) custom-call(bf16[256,1536]{1,0:T(8,128)(2,1)} %bitcast.15, bf16[256,1536]{1,0:T(8,128)(2,1)} %bitcast.16, s32[1,256]{1,0:T(1,128)} %bitcast.19, s32[2,256]{1,0:T(2,128)} %bitcast.18, s32[12,32]{1,0:T(8,128)} %bitcast.17, f32[8,8]{1,0:T(8,128)} %times.1, ...), custom_call_target="tpu_custom_call" | custom-call | tf_op jit(solution)/shard_map/calibrate_and_fill/pallas_call | solution.py:454
  116.5 0.0 copy-start
  116.5 7.6 %copy_out.1 = f32[8400,128]{1,0:T(8,128)} custom-call(f32[8400,128]{1,0:T(8,128)} %get-tuple-element.4.a), custom_call_target="tpu_custom_call" | custom-call | tf_op jit(solution)/shard_map/copy_out/pallas_call | solution.py:503
  124.1 0.0 copy-done
  124.1 1.7 %copy.13 = f32[2,32,8,1536]{3,2,1,0:T(8,128)} copy(f32[2,32,8,1536]{3,2,1,0:T(8,128)S(1)} %bitcast.13) | data formatting | bytes 6291456
Async XLA Ops:
  116.5 7.6 %copy-start = (f32[6144,128]{1,0:T(8,128)S(1)}, f32[6144,128]{1,0:T(8,128)}, u32[]{:S(2)}) copy-start(f32[6144,128]{1,0:T(8,128)} %get-tuple-element.5) | copy-start | bytes 9437188
where the time goes:
time: 126 us
  Pallas kernels  123 us (98%)
  local copies, waits for them, and re-layouts  1.67 us (1%)
    pallas_call x1, Pallas kernels, calibrate_and_fill(): pl.pallas_call(whole_kernel, name='calibrate_and_fill', out_shape=(jax.Sh...  116 us
    pallas_call x1, Pallas kernels, copy_out(): pl.pallas_call(copy_kernel, name='copy_out', grid=(10,), out_shape=jax.Sh...  7.62 us

commit v1 on v0

--- a/solution.py
+++ b/solution.py
@@ -34,6 +34,7 @@
 WINDOW = 8 * TILE
 EDGE = REACH * TILE
 LINE = 2 * BASE
+MINE = PARTS * OWN
 
 
 def nt(a, b, precision=None):
@@ -71,7 +72,7 @@
 
 def whole_kernel(
     amp, ph, group_row, couples, flags, times, channel, inverse, gains, filled,
-    send, got, index, got_index, hot, inv, total, sums, count, shared,
+    send, got, index, got_index, inv, total, shared,
     g_full, g_high, g_low, select, combo, wide, keep, keep_wide, masked, rden, mixed,
     out_cal, in_cal,
     index_send, index_recv, data_send, data_recv, b1_send, b1_recv, b2_send, b2_recv,
@@ -107,11 +108,9 @@
             index, got_index.at[j], index_send.at[j], index_recv.at[j], "bl", peer_of(j)
         )
 
-    def data_copy(n, j):
+    def data_copy(j):
         peer = peer_of(j)
-        return remote(
-            send.at[n, peer], got.at[n, j], data_send.at[n, j], data_recv.at[n, j], "bl", peer
-        )
+        return remote(send.at[peer], got.at[j], data_send.at[j], data_recv.at[j], "bl", peer)
 
     def cal_copy(n, j):
         peer = time_peer(j)
@@ -162,9 +161,9 @@
 
     def turn(n):
         cols = slice(n * CW, (n + 1) * CW)
-        send[n, :, 0:OWN, :] = amp[:, cols].T.reshape(NBL, OWN, ROWS)
-        send[n, :, OWN:2 * OWN, :] = ph[:, cols].T.reshape(NBL, OWN, ROWS)
-        got[n, 0] = send[n, me]
+        for s, ref in enumerate((amp, ph)):
+            first = s * MINE + n * OWN
+            send[:, first:first + OWN, :] = ref[:, cols].T.reshape(NBL, OWN, ROWS)
 
     index[...] = jnp.concatenate(
         [
@@ -172,7 +171,8 @@
             for ref, k in ((group_row, 0), (couples, 0), (couples, 1)) for h in (0, 1)
         ] + [jnp.zeros((2, TILE), I32)], axis=0
     ).astype(I16)
-    turn(0)
+    for n in range(PARTS):
+        turn(n)
     pl.semaphore_wait(barrier, NBL - 1 + NTA - 1)
 
     @pl.loop(1, NBL)
@@ -181,11 +181,9 @@
 
     @pl.loop(1, NBL)
     def _(j):
-        data_copy(0, j).start()
-
-    turn(1)
-    turn(2)
-
+        data_copy(j).start()
+
+    got[0] = send[me]
     got_index[0] = index[...]
     inv[...] = jnp.zeros_like(inv)
     for s in (0, 1):
@@ -219,53 +217,39 @@
 
     clear(total)
 
-    def add_sums(n, low, high):
-        @pl.loop(low, high)
+    def add_sums():
+        @pl.loop(0, NBL)
         def _(j):
             @pl.when(j > 0)
             def _():
-                if n == 0:
-                    index_copy(j).wait_recv()
-                data_copy(n, j).wait_recv()
-                if n + 1 < PARTS:
-                    data_copy(n + 1, j).start()
-
-            d = got[n, j]
-            if n == 0:
-                ix = got_index[j].astype(I32)
-
-                def one_hot(k, size):
-                    row = jnp.concatenate([ix[2 * k:2 * k + 1], ix[2 * k + 1:2 * k + 2]], axis=1)
-                    return (lax.broadcasted_iota(I32, (size, ROWS), 0) == row).astype(F32)
-
-                group = one_hot(0, NGRP).astype(BF16)
-                one, two = one_hot(1, A8), one_hot(2, A8)
-                plus = (one + two).astype(BF16)
-                minus = (one - two).astype(BF16)
-                hot[j, 0:NGRP] = group
-                hot[j, NGRP:NGRP + A8] = plus
-                hot[j, NGRP + A8:HOT] = minus
-                total[...] += nt(hot[j], jnp.concatenate([group, d], axis=0))
-            else:
-                sums[...] += nt(hot[j], d)
-
-    def solve(n):
-        if n == 0:
-            sums[...] = total[:, NGRP:NGRP + 2 * OWN]
-            count[...] = jnp.broadcast_to(
-                jnp.sum(total[0:NGRP, 0:NGRP], axis=1, keepdims=True), (NGRP, 2 * OWN)
+                index_copy(j).wait_recv()
+                data_copy(j).wait_recv()
+
+            ix = got_index[j].astype(I32)
+
+            def one_hot(k, size):
+                row = jnp.concatenate([ix[2 * k:2 * k + 1], ix[2 * k + 1:2 * k + 2]], axis=1)
+                return (lax.broadcasted_iota(I32, (size, ROWS), 0) == row).astype(F32)
+
+            group = one_hot(0, NGRP).astype(BF16)
+            one, two = one_hot(1, A8), one_hot(2, A8)
+            hot = jnp.concatenate(
+                [group, (one + two).astype(BF16), (one - two).astype(BF16)], axis=0
             )
-        mean = sums[0:NGRP] / count[...]
+            total[...] += nt(hot, jnp.concatenate([group, got[j]], axis=0))
+
+    def solve():
+        count = jnp.sum(total[0:NGRP, 0:NGRP], axis=1, keepdims=True)
+        mean = total[0:NGRP, NGRP:NGRP + 2 * MINE] / count
         for s in (0, 1):
             rows = slice(NGRP + s * A8, NGRP + (s + 1) * A8)
-            cols = slice(s * OWN, (s + 1) * OWN)
-            rhs = sums[rows, cols] - jnp.dot(
+            cols = slice(s * MINE, (s + 1) * MINE)
+            rhs = total[rows, NGRP + s * MINE:NGRP + (s + 1) * MINE] - jnp.dot(
                 total[rows, 0:NGRP], mean[:, cols], precision=HIGH, preferred_element_type=F32
             )
-            g = nt(rhs.T, inv[s], HIGH)
-            shared[n, mx, mz, :, s * APAD:(s + 1) * APAD] = encode(g).astype(I16)
-        if n + 1 < PARTS:
-            clear(sums)
+            coded = encode(nt(rhs.T, inv[s], HIGH)).astype(I16)
+            for n in range(PARTS):
+                shared[n, mx, mz, :, s * APAD:(s + 1) * APAD] = coded[n * OWN:(n + 1) * OWN]
 
     started = []
 
@@ -281,13 +265,15 @@
 
     def spread_near(n):
         for sign in (-1, 1):
+            b1_wait(n, sign)
+            for way in (0, 1):
+                begin(b2(n, way, sign, mx))
+        for sign in (-1, 1):
             b1_wait(n, 2 * sign)
             begin(b1(n, 2 * sign, -sign))
             begin(b1(n, 2 * sign, -2 * sign, half=0 if sign < 0 else 1))
-            b1_wait(n, sign)
-        for dz in (-1, 1, -2, 2):
             for way in (0, 1):
-                begin(b2(n, way, dz, mx))
+                begin(b2(n, way, 2 * sign, mx))
 
     def spread_far(n):
         for dz in (-3, 3):
@@ -332,8 +318,9 @@
             cols = slice(s * APAD, (s + 1) * APAD)
             combo[s] = nt(select[s], g_high[:, cols]) + nt(select[s], g_low[:, cols])
 
-        @pl.loop(0, NTA)
-        def _(d):
+        @pl.loop(1, NTA + 1)
+        def _(j):
+            d = time_peer(j)
             rows = pl.ds(pl.multiple_of(d * BASE, BASE), BASE)
             cols = slice(n * CW, (n + 1) * CW)
             u = amp[rows, cols].astype(F32) - combo[0, rows, :]
@@ -343,9 +330,9 @@
             out_cal[n, d, 0] = (magnitude * cosine).astype(BF16)
             out_cal[n, d, 1] = (magnitude * sine).astype(BF16)
 
-        @pl.loop(1, NTA)
-        def _(j):
-            cal_copy(n, j).start()
+            @pl.when(j < NTA)
+            def _():
+                cal_copy(n, j).start()
 
         in_cal[n, 0] = out_cal[n, mt]
         for s in (0, 1):
@@ -396,35 +383,24 @@
                             result[:, i * TILE:(i + 1) * TILE]
                         )
 
-    add_sums(0, 0, NBL)
-    solve(0)
-    spread_start(0)
-    add_sums(1, 0, 8)
+    add_sums()
+    solve()
+    for n in range(PARTS):
+        spread_start(n)
     spread_near(0)
-    add_sums(1, 8, 16)
+    spread_near(1)
     spread_far(0)
-    add_sums(1, 16, 24)
+    spread_near(2)
+    spread_far(1)
     spread_across(0)
-    add_sums(1, 24, NBL)
-    solve(1)
-    spread_start(1)
+    spread_far(2)
+    spread_across(1)
     spread_end(0)
-    add_sums(2, 0, 8)
-    spread_near(1)
     calibrate(0)
-    add_sums(2, 8, 16)
-    spread_far(1)
-    add_sums(2, 16, 24)
-    spread_across(1)
-    add_sums(2, 24, NBL)
-    solve(2)
-    spread_start(2)
+    spread_across(2)
     spread_end(1)
+    calibrate(1)
     mask(0)
-    spread_near(2)
-    calibrate(1)
-    spread_far(2)
-    spread_across(2)
     mask(1)
     fill(0, 2)
     spread_end(2)
@@ -438,8 +414,7 @@
     @pl.loop(1, NBL)
     def _(j):
         index_copy(j).wait_send()
-        for n in range(PARTS):
-            data_copy(n, j).wait_send()
+        data_copy(j).wait_send()
 
     @pl.loop(1, NTA)
     def _(j):
@@ -461,15 +436,12 @@
         in_specs=[vmem] * 5 + [smem, vmem, vmem],
         out_specs=(vmem, vmem),
         scratch_shapes=[
-            pltpu.VMEM((PARTS, NBL, 2 * OWN, ROWS), BF16),
-            pltpu.VMEM((PARTS, NBL, 2 * OWN, ROWS), BF16),
+            pltpu.VMEM((NBL, 2 * MINE, ROWS), BF16),
+            pltpu.VMEM((NBL, 2 * MINE, ROWS), BF16),
             pltpu.VMEM((8, 128), I16),
             pltpu.VMEM((NBL, 8, 128), I16),
-            pltpu.VMEM((NBL, HOT, ROWS), BF16),
             pltpu.VMEM((2, APAD, A8), F32),
-            pltpu.VMEM((HOT, NGRP + 2 * OWN), F32),
-            pltpu.VMEM((HOT, 2 * OWN), F32),
-            pltpu.VMEM((NGRP, 2 * OWN), F32),
+            pltpu.VMEM((HOT, NGRP + 2 * MINE), F32),
             pltpu.VMEM((PARTS, NX, NZ, OWN, 2 * APAD), I16),
             pltpu.VMEM((CW, 2 * APAD), F32),
             pltpu.VMEM((CW, 2 * APAD), BF16),
@@ -484,30 +456,41 @@
             pltpu.VMEM((NT * LINE, PAIR), F32),
             pltpu.VMEM((PARTS, NTA, 2, BASE, CW), BF16),
             pltpu.VMEM((PARTS, NTA, 2, BASE, CW), BF16),
-            dma((NBL,)), dma((NBL,)), dma((PARTS, NBL)), dma((PARTS, NBL)),
+            dma((NBL,)), dma((NBL,)), dma((NBL,)), dma((NBL,)),
             dma((PARTS, NZ)), dma((PARTS, NZ)), dma((PARTS, 2, NZ)), dma((PARTS, 2, NZ)),
             dma((PARTS, NZ)), dma((PARTS, NZ)), dma((PARTS, NTA)), dma((PARTS, NTA)),
         ],
         compiler_params=pltpu.CompilerParams(
-            collective_id=0, has_side_effects=True, vmem_limit_bytes=56 * 2**20
+            collective_id=0, has_side_effects=True, vmem_limit_bytes=40 * 2**20
         ),
     )(amp, ph, group_row, couples, flags, times, channel, inverse)
 
 
-def copy_kernel(a, out):
-    out[...] = a[...]
-
-
-def copy_out(a):
-    spec = pl.BlockSpec((a.shape[0] // 10, TILE), lambda i: (i, 0))
+def copy_kernel(a, b, out_a, out_b, sem):
+    copies = []
+    for k, (src, dst) in enumerate(((a, out_a), (b, out_b))):
+        size = src.shape[0] // 2
+        for i in range(2):
+            rows = pl.ds(i * size, size)
+            copies.append(pltpu.make_async_copy(src.at[rows], dst.at[rows], sem.at[k, i]))
+    for copy in copies:
+        copy.start()
+    for copy in copies:
+        copy.wait()
+
+
+def copy_out(a, b):
     return pl.pallas_call(
         copy_kernel,
         name="copy_out",
-        grid=(10,),
-        out_shape=jax.ShapeDtypeStruct(a.shape, a.dtype),
-        in_specs=[spec],
-        out_specs=spec,
-    )(a)
+        out_shape=(
+            jax.ShapeDtypeStruct(a.shape, a.dtype), jax.ShapeDtypeStruct(b.shape, b.dtype)
+        ),
+        in_specs=[pl.BlockSpec(memory_space=pltpu.VMEM)] * 2,
+        out_specs=(pl.BlockSpec(memory_space=pl.ANY),) * 2,
+        scratch_shapes=[pltpu.SemaphoreType.DMA((2, 2))],
+        compiler_params=pltpu.CompilerParams(vmem_limit_bytes=10 * 2**20),
+    )(a, b)
 
 
 def on_device(
@@ -520,11 +503,10 @@
     integration_kernel,
     channel_kernel,
 ):
-    gains, filled = calibrate_and_fill(
+    gains, filled = copy_out(*calibrate_and_fill(
         log_amplitude[:, 0], phase[:, 0], redundant_group_index[None, :], antenna_couples.T,
         tile_flag_mask.T, integration_kernel, channel_kernel, inverse.transpose(1, 0, 2),
-    )
-    gains = copy_out(gains)
+    ))
     return (
         gains.reshape(2, ANTENNA_COUNT, 1, CH),
         filled.reshape(2, BASE, NTILE, NT, TILE).transpose(0, 1, 3, 2, 4).reshape(2, BASE, NT, CH),

time: 126 us -> 118 us (0.937)
  Pallas kernels: 123 us -> 110 us
  local copies, waits for them, and re-layouts: 1.67 us -> 7.17 us
    pallas_call x1, Pallas kernels: 116 us -> 107 us  [calibrate_and_fill(): pl.pallas_call(whole_kernel, name='calibrate_and_fill', out_shape=(jax.Sh...]
    unnamed x3 -> x16, local copies, waits for them, and re-layouts: 1.67 us -> 7.17 us
    pallas_call x1, Pallas kernels: 7.62 us -> 3.07 us  [copy_out(): pl.pallas_call(copy_kernel, name='copy_out', out_shape=(jax.ShapeDtypeStr...]
where the time goes in v1:
time: 118 us
  Pallas kernels  110 us (93%)
  local copies, waits for them, and re-layouts  7.17 us (6%)
    pallas_call x1, Pallas kernels, calibrate_and_fill(): pl.pallas_call(whole_kernel, name='calibrate_and_fill', out_shape=(jax.Sh...  107 us
    unnamed x16, local copies, waits for them, and re-layouts  7.17 us
    pallas_call x1, Pallas kernels, copy_out(): pl.pallas_call(copy_kernel, name='copy_out', out_shape=(jax.ShapeDtypeStr...  3.07 us

profile of v1, /device:TPU:1, one launch (start us, length us, event | category | flops | bytes accessed | tf_op | source)
XLA Modules:
  0.0 117.8 jit_solution(12765743518587097024)
XLA Ops:
  0.6 0.0 copy-start
  0.6 1.2 %copy-done = f32[2,350,350]{2,0,1:T(2,128)S(1)} copy-done((f32[2,350,350]{2,0,1:T(2,128)S(1)}, f32[2,350,350]{2,0,1:T(2,128)}, u32[]{:S(2)}) %copy-start) | copy-done | bytes 980024
  1.9 0.0 copy-start.1
  1.9 1.1 copy-done.1
  3.0 0.0 copy-start.2
  3.0 1.1 copy-done.2
  4.1 0.0 copy-start.3
  4.1 0.9 copy-done.3
  5.1 0.0 copy-start.4
  5.1 0.7 copy-done.4
  5.8 0.0 copy-start.5
  5.8 0.7 copy-done.5
  6.5 0.0 copy-start.6
  6.5 0.7 copy-done.6
  7.1 0.0 copy-start.7
  7.1 0.7 copy-done.7
  7.8 106.9 %calibrate_and_fill.1 = (f32[8400,128]{1,0:T(8,128)S(1)}, f32[6144,128]{1,0:T(8,128)S(1)}) custom-call(bf16[256,1536]{1,0:T(8,128)(2,1)S(1)} %bitcast.13, bf16[256,1536]{1,0:T(8,128)(2,1)S(1)} %bitcast.14, s32[1,256]{1,0:T(1,128)S(1)} %bitcast.17, s32[2,256]{1,0:T(2,128)S(1)} %bitcast.16, s32[12,32]{1,0:T(8,128)S(1)} %bitcast.15, f32[8,8]{1,0:T(8,128)S(1)} %copy-done.5, ...), custom_call_target="tpu_custom_call" | custom-call | tf_op jit(solution)/shard_map/calibrate_and_fill/pallas_call | solution.py:429
  114.7 3.1 %copy_out.1 = (f32[8400,128]{1,0:T(8,128)}, f32[6144,128]{1,0:T(8,128)}) custom-call(f32[8400,128]{1,0:T(8,128)S(1)} %get-tuple-element.6.a, f32[6144,128]{1,0:T(8,128)S(1)} %get-tuple-element.7.b), custom_call_target="tpu_custom_call" | custom-call | tf_op jit(solution)/shard_map/copy_out/pallas_call | solution.py:483
Async XLA Ops:
  0.6 1.2 %copy-start = (f32[2,350,350]{2,0,1:T(2,128)S(1)}, f32[2,350,350]{2,0,1:T(2,128)}, u32[]{:S(2)}) copy-start(f32[2,350,350]{2,0,1:T(2,128)} %param.13) | copy-start | bytes 2940004
  1.9 1.1 copy-start.1
  3.0 1.1 copy-start.2
  4.1 0.9 copy-start.3
  5.1 0.7 copy-start.4
  5.8 0.7 copy-start.5
  6.5 0.7 copy-start.6
  7.1 0.7 copy-start.7

commit v2 on v1

--- a/solution.py
+++ b/solution.py
@@ -71,8 +71,8 @@
 
 
 def whole_kernel(
-    amp, ph, group_row, couples, flags, times, channel, inverse, gains, filled,
-    send, got, index, got_index, inv, total, shared,
+    amp_in, ph_in, group_in, couples_in, flags_in, times_in, channel_in, inverse_in, gains, filled,
+    amp, ph, group_row, couples, flags, times, channel, inverse, in_sem, send, got, index, got_index, inv, total, shared,
     g_full, g_high, g_low, select, combo, wide, keep, keep_wide, masked, rden, mixed,
     out_cal, in_cal,
     index_send, index_recv, data_send, data_recv, b1_send, b1_recv, b2_send, b2_recv,
@@ -149,6 +149,15 @@
             slot, slot, b3_send.at[n, number], b3_recv.at[n, number], "bl", device(1 - 2 * way, 0)
         )
 
+    incoming = [
+        pltpu.make_async_copy(src, dst, in_sem.at[k])
+        for k, (src, dst) in enumerate((
+            (amp_in, amp), (ph_in, ph), (group_in, group_row), (couples_in, couples),
+            (flags_in, flags), (times_in, times), (channel_in, channel), (inverse_in, inverse),
+        ))
+    ]
+    for copy in incoming:
+        copy.start()
     barrier = pltpu.get_barrier_semaphore()
 
     @pl.loop(1, NBL)
@@ -165,6 +174,8 @@
             first = s * MINE + n * OWN
             send[:, first:first + OWN, :] = ref[:, cols].T.reshape(NBL, OWN, ROWS)
 
+    for copy in incoming[:4]:
+        copy.wait()
     index[...] = jnp.concatenate(
         [
             ref[k:k + 1, h * TILE:(h + 1) * TILE]
@@ -183,6 +194,8 @@
     def _(j):
         data_copy(j).start()
 
+    for copy in incoming[4:]:
+        copy.wait()
     got[0] = send[me]
     got_index[0] = index[...]
     inv[...] = jnp.zeros_like(inv)
@@ -425,7 +438,7 @@
 def calibrate_and_fill(amp, ph, group_row, couples, flags, times, channel, inverse):
     dma = pltpu.SemaphoreType.DMA
     vmem = pl.BlockSpec(memory_space=pltpu.VMEM)
-    smem = pl.BlockSpec(memory_space=pltpu.SMEM)
+    hbm = pl.BlockSpec(memory_space=pltpu.HBM)
     return pl.pallas_call(
         whole_kernel,
         name="calibrate_and_fill",
@@ -433,9 +446,18 @@
             jax.ShapeDtypeStruct((2 * ANTENNA_COUNT * NTILE, TILE), F32),
             jax.ShapeDtypeStruct((2 * BASE * NTILE * NT, TILE), F32),
         ),
-        in_specs=[vmem] * 5 + [smem, vmem, vmem],
+        in_specs=[hbm] * 8,
         out_specs=(vmem, vmem),
         scratch_shapes=[
+            pltpu.VMEM((ROWS, CH), BF16),
+            pltpu.VMEM((ROWS, CH), BF16),
+            pltpu.VMEM((1, ROWS), I32),
+            pltpu.VMEM((2, ROWS), I32),
+            pltpu.VMEM((NTILE, BASE), I32),
+            pltpu.SMEM((NT, NT), F32),
+            pltpu.VMEM((2 * REACH + 1, TILE, TILE), BF16),
+            pltpu.VMEM((ANTENNA_COUNT, 2, ANTENNA_COUNT), F32),
+            dma((8,)),
             pltpu.VMEM((NBL, 2 * MINE, ROWS), BF16),
             pltpu.VMEM((NBL, 2 * MINE, ROWS), BF16),
             pltpu.VMEM((8, 128), I16),
@@ -463,7 +485,10 @@
         compiler_params=pltpu.CompilerParams(
             collective_id=0, has_side_effects=True, vmem_limit_bytes=40 * 2**20
         ),
-    )(amp, ph, group_row, couples, flags, times, channel, inverse)
+    )(*(
+        pltpu.with_memory_space_constraint(x, pltpu.HBM)
+        for x in (amp, ph, group_row, couples, flags, times, channel, inverse)
+    ))
 
 
 def copy_kernel(a, b, out_a, out_b, sem):

time: 118 us -> 110 us (0.932)
  local copies, waits for them, and re-layouts: 7.17 us -> 0 us
    unnamed x16 -> x0, local copies, waits for them, and re-layouts: 7.17 us -> none
where the time goes in v2:
time: 110 us
  Pallas kernels  110 us (100%)
    pallas_call x1, Pallas kernels, calibrate_and_fill(): pl.pallas_call(whole_kernel, name='calibrate_and_fill', out_shape=(jax.Sh...  106 us
    pallas_call x1, Pallas kernels, copy_out(): pl.pallas_call(copy_kernel, name='copy_out', out_shape=(jax.ShapeDtypeStr...  3.07 us

profile of v2, /device:TPU:1, one launch (start us, length us, event | category | flops | bytes accessed | tf_op | source)
XLA Modules:
  0.0 110.2 jit_solution(12320776433157280558)
XLA Ops:
  0.6 106.5 %calibrate_and_fill.1 = (f32[8400,128]{1,0:T(8,128)S(1)}, f32[6144,128]{1,0:T(8,128)S(1)}) custom-call(bf16[256,1536]{1,0:T(8,128)(2,1)} %bitcast.13, bf16[256,1536]{1,0:T(8,128)(2,1)} %bitcast.14, s32[1,256]{1,0:T(1,128)} %bitcast.17, s32[2,256]{1,0:T(2,128)} %bitcast.16, s32[12,32]{1,0:T(8,128)} %bitcast.15, f32[8,8]{1,0:T(8,128)} %times_in.1, ...), custom_call_target="tpu_custom_call" | custom-call | tf_op jit(solution)/shard_map/calibrate_and_fill/pallas_call | solution.py:442
  107.1 3.1 %copy_out.1 = (f32[8400,128]{1,0:T(8,128)}, f32[6144,128]{1,0:T(8,128)}) custom-call(f32[8400,128]{1,0:T(8,128)S(1)} %get-tuple-element.6.a, f32[6144,128]{1,0:T(8,128)S(1)} %get-tuple-element.7.b), custom_call_target="tpu_custom_call" | custom-call | tf_op jit(solution)/shard_map/copy_out/pallas_call | solution.py:508

commit v3 on v2

--- a/solution.py
+++ b/solution.py
@@ -323,7 +323,7 @@
                 k = part[:, ANTENNA_COUNT:ANTENNA_COUNT + 1] - 15
                 g = part.astype(F32) * jnp.exp2(k.astype(F32))
                 high = g.astype(BF16)
-                g_full[rows, cols] = g
+                g_full[n, rows, cols] = g
                 g_high[rows, cols] = high
                 g_low[rows, cols] = (g - high.astype(F32)).astype(BF16)
 
@@ -348,10 +348,13 @@
                 cal_copy(n, j).start()
 
         in_cal[n, 0] = out_cal[n, mt]
+
+    def write_gains(n):
         for s in (0, 1):
             @pl.loop(0, CW // TILE)
             def _(k):
-                block = g_full[pl.ds(pl.multiple_of(k * TILE, TILE), TILE), s * APAD:(s + 1) * APAD]
+                rows = pl.ds(pl.multiple_of(k * TILE, TILE), TILE)
+                block = g_full[n, rows, s * APAD:(s + 1) * APAD]
                 start = s * ANTENNA_COUNT * NTILE + n * (CW // TILE) + k
                 gains[pl.ds(start, ANTENNA_COUNT, stride=NTILE), :] = block.T[0:ANTENNA_COUNT]
 
@@ -413,11 +416,14 @@
     spread_across(2)
     spread_end(1)
     calibrate(1)
+    spread_end(2)
+    calibrate(2)
+    write_gains(0)
     mask(0)
+    write_gains(1)
     mask(1)
     fill(0, 2)
-    spread_end(2)
-    calibrate(2)
+    write_gains(2)
     mask(2)
     fill(2, NTILE // 2)
 
@@ -465,7 +471,7 @@
             pltpu.VMEM((2, APAD, A8), F32),
             pltpu.VMEM((HOT, NGRP + 2 * MINE), F32),
             pltpu.VMEM((PARTS, NX, NZ, OWN, 2 * APAD), I16),
-            pltpu.VMEM((CW, 2 * APAD), F32),
+            pltpu.VMEM((PARTS, CW, 2 * APAD), F32),
             pltpu.VMEM((CW, 2 * APAD), BF16),
             pltpu.VMEM((CW, 2 * APAD), BF16),
             pltpu.VMEM((2, ROWS, APAD), BF16),

time: 110 us -> 105 us (0.955)
  Pallas kernels: 110 us -> 104 us
    pallas_call x1, Pallas kernels: 106 us -> 101 us  [calibrate_and_fill(): pl.pallas_call(whole_kernel, name='calibrate_and_fill', out_shape=(jax.Sh...]
where the time goes in v3:
time: 105 us
  Pallas kernels  104 us (99%)
    pallas_call x1, Pallas kernels, calibrate_and_fill(): pl.pallas_call(whole_kernel, name='calibrate_and_fill', out_shape=(jax.Sh...  101 us
    pallas_call x1, Pallas kernels, copy_out(): pl.pallas_call(copy_kernel, name='copy_out', out_shape=(jax.ShapeDtypeStr...  3.07 us

profile of v3, /device:TPU:1, one launch (start us, length us, event | category | flops | bytes accessed | tf_op | source)
XLA Modules:
  0.0 104.8 jit_solution(7758166912624164934)
XLA Ops:
  0.6 101.1 %calibrate_and_fill.1 = (f32[8400,128]{1,0:T(8,128)S(1)}, f32[6144,128]{1,0:T(8,128)S(1)}) custom-call(bf16[256,1536]{1,0:T(8,128)(2,1)} %bitcast.13, bf16[256,1536]{1,0:T(8,128)(2,1)} %bitcast.14, s32[1,256]{1,0:T(1,128)} %bitcast.17, s32[2,256]{1,0:T(2,128)} %bitcast.16, s32[12,32]{1,0:T(8,128)} %bitcast.15, f32[8,8]{1,0:T(8,128)} %times_in.1, ...), custom_call_target="tpu_custom_call" | custom-call | tf_op jit(solution)/shard_map/calibrate_and_fill/pallas_call | solution.py:448
  101.7 3.1 %copy_out.1 = (f32[8400,128]{1,0:T(8,128)}, f32[6144,128]{1,0:T(8,128)}) custom-call(f32[8400,128]{1,0:T(8,128)S(1)} %get-tuple-element.6.a, f32[6144,128]{1,0:T(8,128)S(1)} %get-tuple-element.7.b), custom_call_target="tpu_custom_call" | custom-call | tf_op jit(solution)/shard_map/copy_out/pallas_call | solution.py:514

commit v4 on v3

--- a/solution.py
+++ b/solution.py
@@ -74,7 +74,7 @@
     amp_in, ph_in, group_in, couples_in, flags_in, times_in, channel_in, inverse_in, gains, filled,
     amp, ph, group_row, couples, flags, times, channel, inverse, in_sem, send, got, index, got_index, inv, total, shared,
     g_full, g_high, g_low, select, combo, wide, keep, keep_wide, masked, rden, mixed,
-    out_cal, in_cal,
+    early, out_cal, in_cal,
     index_send, index_recv, data_send, data_recv, b1_send, b1_recv, b2_send, b2_recv,
     b3_send, b3_recv, cal_send, cal_recv,
 ):
@@ -372,11 +372,19 @@
                     in_cal[n, j, c] * w
                 )
 
+    known = {2: 3 * PAIR, 3: 2 * PAIR, 4: PAIR}
+
+    def fill_known():
+        for p, size in known.items():
+            early[p - 2] = nt(masked[:, p * PAIR:p * PAIR + size], wide[:, 0:size])
+
     def fill(low, high):
-        @pl.loop(low, high)
-        def _(p):
-            lane = pl.multiple_of(p * PAIR, PAIR)
-            mixed[...] = nt(masked[:, pl.ds(lane, WINDOW)], wide[...])
+        for p in range(low, high):
+            lane = p * PAIR
+            size = known.get(p, 0) if high > 2 else 0
+            stop = 3 * PAIR if p == NTILE // 2 - 1 else WINDOW
+            rest = nt(masked[:, lane + size:lane + stop], wide[:, size:stop])
+            mixed[...] = early[p - 2] + rest if size else rest
 
             @pl.loop(0, NT)
             def _(to):
@@ -389,7 +397,7 @@
                 w = keep[:, pl.ds(lane, PAIR)]
                 for c in (0, 1):
                     row = pl.multiple_of(to * LINE + c * BASE, BASE)
-                    own = masked[pl.ds(row, BASE), pl.ds(pl.multiple_of(lane + EDGE, TILE), PAIR)]
+                    own = masked[pl.ds(row, BASE), pl.ds(lane + EDGE, PAIR)]
                     result = jnp.where(
                         w > 0.5, own.astype(F32), value[c * BASE:(c + 1) * BASE] * ratio
                     )
@@ -424,6 +432,7 @@
     mask(1)
     fill(0, 2)
     write_gains(2)
+    fill_known()
     mask(2)
     fill(2, NTILE // 2)
 
@@ -482,6 +491,7 @@
             pltpu.VMEM((NT * LINE, CH + 2 * EDGE), BF16),
             pltpu.VMEM((BASE, CH), F32),
             pltpu.VMEM((NT * LINE, PAIR), F32),
+            pltpu.VMEM((3, NT * LINE, PAIR), F32),
             pltpu.VMEM((PARTS, NTA, 2, BASE, CW), BF16),
             pltpu.VMEM((PARTS, NTA, 2, BASE, CW), BF16),
             dma((NBL,)), dma((NBL,)), dma((NBL,)), dma((NBL,)),

time: 105 us -> 106 us (level)
  no operation moved by 1% of the time
where the time goes in v4:
time: 106 us
  Pallas kernels  105 us (99%)
    pallas_call x1, Pallas kernels, calibrate_and_fill(): pl.pallas_call(whole_kernel, name='calibrate_and_fill', out_shape=(jax.Sh...  102 us
    pallas_call x1, Pallas kernels, copy_out(): pl.pallas_call(copy_kernel, name='copy_out', out_shape=(jax.ShapeDtypeStr...  3.07 us

profile of v4, /device:TPU:1, one launch (start us, length us, event | category | flops | bytes accessed | tf_op | source)
XLA Modules:
  0.0 105.7 jit_solution(16660894681468984062)
XLA Ops:
  0.6 102.0 %calibrate_and_fill.1 = (f32[8400,128]{1,0:T(8,128)S(1)}, f32[6144,128]{1,0:T(8,128)S(1)}) custom-call(bf16[256,1536]{1,0:T(8,128)(2,1)} %bitcast.13, bf16[256,1536]{1,0:T(8,128)(2,1)} %bitcast.14, s32[1,256]{1,0:T(1,128)} %bitcast.17, s32[2,256]{1,0:T(2,128)} %bitcast.16, s32[12,32]{1,0:T(8,128)} %bitcast.15, f32[8,8]{1,0:T(8,128)} %times_in.1, ...), custom_call_target="tpu_custom_call" | custom-call | tf_op jit(solution)/shard_map/calibrate_and_fill/pallas_call | solution.py:457
  102.7 3.1 %copy_out.1 = (f32[8400,128]{1,0:T(8,128)}, f32[6144,128]{1,0:T(8,128)}) custom-call(f32[8400,128]{1,0:T(8,128)S(1)} %get-tuple-element.6.a, f32[6144,128]{1,0:T(8,128)S(1)} %get-tuple-element.7.b), custom_call_target="tpu_custom_call" | custom-call | tf_op jit(solution)/shard_map/copy_out/pallas_call | solution.py:524
